TPU v7x, 256 devices: a whole 4x4x8 slice. The times are simulated.
256 devices in a mesh: ctx: 32 (over x, y, z_lo), tp: 8 (over z_hi, core).
Axes of the slice: x: 4, y: 4, z: 8 (z_hi: 4, z_lo: 2; z = z_hi * 2 + z_lo), core: 2. Of those that a mesh axis runs over, the one named last changes fastest.
Arguments:
- features: bfloat16 [8192, 8192], P('ctx', 'tp'), may hold values from -6 to 6
- inner: bfloat16 [8192, 8192], P('ctx', 'tp'), may hold values from -6 to 6
- w_bc: bfloat16 [8192, 2, 1024], P('ctx', None, 'tp'), may hold values from -0.005859375 to 0.005859375
- w_dt: bfloat16 [8192, 128], P('ctx', 'tp'), may hold values from -0.0625 to 0.0625
- dt_bias: float32 [128], P('tp'), may hold values from -4 to 0
- decay_rate: float32 [128], P('tp'), may hold values from 0.00012207031 to 1
- skip: float32 [128], P('tp'), may hold values from 0.5 to 1.5
- cotangent: bfloat16 [8192, 8192], P('ctx', 'tp'), may hold values from -6 to 6
- fisher: float32 [8192, 2, 1024], P('ctx', None, 'tp'), may hold values from 0.5 to 4
- importance: float32 [8192, 2, 1024], P('ctx', None, 'tp'), may hold values from 0 to 10
Outputs:
- outputs: bfloat16 [8192, 8192], P('ctx', 'tp')
- grad_inner: bfloat16 [8192, 8192], P('ctx', 'tp')
- grad_features: bfloat16 [8192, 8192], P('ctx', 'tp')
- weight_new: float32 [8192, 2, 1024], P('ctx', None, 'tp')
- fisher_new: float32 [8192, 2, 1024], P('ctx', None, 'tp')
- importance_new: float32 [8192, 2, 1024], P('ctx', None, 'tp')
All inputs are finite; a program needn't handle non-finite values.
Results may differ from a plain program's by a relative error of at most 0.014.
Values may be sent and summed in bfloat16 or wider, within the bound.
A program may use at most 128 MiB of HBM per device.

v0:
```python
from functools import partial
import math
import jax
import jax.numpy as jnp
from jax import lax
from jax.sharding import Mesh
from jax.sharding import PartitionSpec as P

HEADS = 128
P_SIZE = 64
N = 128
G = 8
SPAN = 256
CTX = ("ctx_0", "ctx_1", "ctx_2")
HIGH = lax.Precision.HIGHEST
MIX = 0.25
STEP = 0.1
EPS = 1e-06


def in_one_piece(arrays, axis, dim, along):
    widths = [math.prod(a.shape[along:]) for a in arrays]
    both = jnp.concatenate(
        [a.reshape(*a.shape[:along], w) for a, w in zip(arrays, widths)], axis=along
    )
    whole = lax.all_gather(both, axis, axis=dim, tiled=True)
    blocks = jnp.split(whole, [sum(widths[:k]) for k in range(1, len(widths))], axis=along)
    return tuple(
        (b.reshape(*whole.shape[:along], *a.shape[along:]) for a, b in zip(arrays, blocks))
    )


def nothing_yet(x, identity):
    return jax.tree.map(
        lambda part, zero: jnp.zeros_like(part) + jnp.asarray(zero, part.dtype), x, identity
    )


def prefix_by_axis(x, axes, combine, identity, reverse):
    before = start = nothing_yet(x, identity)
    running = x
    for axis in reversed(axes):
        size, mine = (lax.axis_size(axis), lax.axis_index(axis))
        pieces = jax.tree.map(lambda part: lax.all_gather(part, axis), running)
        inside, running = (start, start)
        for k in reversed(range(size)) if reverse else range(size):
            passed = k > mine if reverse else k < mine
            running = combine(running, jax.tree.map(lambda part: part[k], pieces))
            inside = jax.tree.map(lambda new, old: jnp.where(passed, new, old), running, inside)
        before = combine(inside, before)
    return before


def in_order(blocks, dim):
    shape = list(blocks.shape[1:])
    shape[dim] *= blocks.shape[0]
    return jnp.moveaxis(blocks, 0, dim).reshape(shape)


def gather_together(arrays, axis, dims):
    ravelled = jnp.concatenate([a.reshape(-1) for a in arrays])
    lines, at, gathered = (lax.all_gather(ravelled, axis), 0, [])
    for a, dim in zip(arrays, dims):
        blocks = lines[:, at : at + a.size].reshape(-1, *a.shape)
        gathered.append(in_order(blocks, dim))
        at += a.size
    return tuple(gathered)


def summed_rows(x, axes, dim):
    for axis in axes:
        x = lax.psum_scatter(x, axis, scatter_dimension=dim, tiled=True)
    return x


def span_pass(dt_bias, rate, state, blocks):
    xc, bc, cc, zc = blocks
    dt = jax.nn.softplus(zc + dt_bias)
    logs = -rate * dt
    cums = jnp.cumsum(logs, axis=0)
    length = xc.shape[0]
    rows = lax.broadcasted_iota(jnp.int32, (length, length), 0)
    cols = lax.broadcasted_iota(jnp.int32, (length, length), 1)
    causal = rows >= cols
    scores = jnp.einsum("ign,jgn->gij", cc, bc, precision=HIGH)
    order = jnp.transpose(cums, (1, 2, 0))
    diff = order[:, :, :, None] - order[:, :, None, :]
    decays = jnp.where(causal, jnp.exp(jnp.where(causal, diff, 0.0)), 0.0)
    weights = decays * scores[:, None] * jnp.transpose(dt, (1, 2, 0))[:, :, None, :]
    intra = jnp.einsum("ghij,jghp->ighp", weights, xc, precision=HIGH)
    inter = jnp.exp(cums)[..., None] * jnp.einsum("ign,ghpn->ighp", cc, state, precision=HIGH)
    last = cums[-1]
    tail = jnp.exp(last[None] - cums) * dt
    fresh = jnp.einsum("jghp,jgh,jgn->ghpn", xc, tail, bc, precision=HIGH)
    new_state = jnp.exp(last)[..., None, None] * state + fresh
    return (new_state, intra + inter)


def run_spans(x, b, c, z, dt_bias, rate):
    tokens, groups, heads, width = x.shape
    count = tokens // SPAN
    state0 = jnp.zeros((groups, heads, width, b.shape[-1]), jnp.float32)
    blocks = (
        x.reshape(count, SPAN, groups, heads, width),
        b.reshape(count, SPAN, groups, b.shape[-1]),
        c.reshape(count, SPAN, groups, c.shape[-1]),
        z.reshape(count, SPAN, groups, heads),
    )
    final, ys = lax.scan(partial(span_pass, dt_bias, rate), state0, blocks)
    return (ys.reshape(tokens, groups, heads, width), final)


def link(earlier, later):
    return (earlier[0] * later[0], later[0][..., None, None] * earlier[1] + later[1])


def contract_last(left, right):
    return lax.dot_general(
        left, right, (((1,), (1,)), ((), ())), preferred_element_type=jnp.float32
    )


def rwalk(weight, grad, fisher, importance):
    fisher_new = MIX * grad * grad + (1.0 - MIX) * fisher
    delta = -STEP * grad
    importance_new = importance + -grad * delta / (0.5 * fisher_new * delta * delta + EPS)
    weight_new = weight.astype(jnp.float32) + delta
    return (weight_new, fisher_new, importance_new)


def local(features, inner, w_bc, w_dt, dt_bias, decay_rate, skip, cotangent, fisher, importance):
    tokens = features.shape[0]
    groups = w_bc.shape[2] // N
    per_group = HEADS // G
    whole = lax.all_gather(features, "tp", axis=1, tiled=True)
    rows_bc, rows_dt = in_one_piece((w_bc, w_dt), CTX, 0, 1)
    depth = rows_bc.shape[0]
    wide = rows_bc.reshape(depth, 2 * groups * N)
    block_bc, block_dt = (
        lax.all_to_all(wide, "tp", split_axis=0, concat_axis=1, tiled=True),
        lax.all_to_all(rows_dt, "tp", split_axis=0, concat_axis=1, tiled=True),
    )
    proj = jnp.dot(whole, wide, preferred_element_type=jnp.float32)
    proj = lax.optimization_barrier(proj.astype(jnp.bfloat16)).astype(jnp.float32)
    bmat = proj[:, : groups * N].reshape(tokens, groups, N)
    cmat = proj[:, groups * N :].reshape(tokens, groups, N)
    zdt = jnp.dot(whole, rows_dt, preferred_element_type=jnp.float32).reshape(
        tokens, groups, per_group
    )
    bias = dt_bias.reshape(groups, per_group)
    rate = decay_rate.reshape(groups, per_group)
    gain = skip.reshape(groups, per_group)
    xval = inner.astype(jnp.float32).reshape(tokens, groups, per_group, P_SIZE)

    def zero_start(xv, bv, cv, zv):
        core, final = run_spans(xv, bv, cv, zv, bias, rate)
        return (core + gain[..., None] * xv, final)

    def enter(cv, zv, incoming):
        logs = -rate * jax.nn.softplus(zv + bias)
        cums = jnp.cumsum(logs, axis=0)
        added = jnp.exp(cums)[..., None] * jnp.einsum(
            "ign,ghpn->ighp", cv, incoming, precision=HIGH
        )
        return (added, jnp.exp(cums[-1])[..., None, None] * incoming)

    (base, local_state), back_zero = jax.vjp(zero_start, xval, bmat, cmat, zdt)
    decay = jnp.exp(jnp.sum(-rate * jax.nn.softplus(zdt + bias), axis=0))
    identity = (jnp.ones_like(decay), jnp.zeros_like(local_state))
    carried = prefix_by_axis((decay, local_state), CTX, link, identity, False)[1]
    (added, passed), back_enter = jax.vjp(enter, cmat, zdt, carried)
    outputs = (base + added).reshape(tokens, -1).astype(jnp.bfloat16)
    upstream = cotangent.astype(jnp.float32).reshape(xval.shape)
    dc_enter, dz_enter, state_local = back_enter((upstream, jnp.zeros_like(passed)))
    later = prefix_by_axis((decay, state_local), CTX, link, identity, True)[1]
    dz_pass = back_enter((jnp.zeros_like(upstream), later))[1]
    dx, dbm, dc_zero, dz_zero = back_zero((upstream, later))
    dcm = dc_zero + dc_enter
    dz = dz_zero + dz_enter + dz_pass
    grad_inner = dx.reshape(tokens, -1).astype(jnp.bfloat16)
    dproj = jnp.concatenate(
        [dbm.reshape(tokens, groups * N), dcm.reshape(tokens, groups * N)], axis=1
    ).astype(jnp.bfloat16)
    dz_half = dz.reshape(tokens, -1).astype(jnp.bfloat16)
    every_bc, every_dt = gather_together((dproj, dz_half), "tp", (1, 1))
    grad_features = (contract_last(every_bc, block_bc) + contract_last(every_dt, block_dt)).astype(
        jnp.bfloat16
    )
    product = lax.dot_general(
        whole, dproj, (((0,), (0,)), ((), ())), preferred_element_type=jnp.float32
    )
    summed = summed_rows(product, CTX, 0)
    grad = summed.reshape(w_bc.shape) / (tokens * lax.axis_size(CTX))
    weight_new, fisher_new, importance_new = rwalk(w_bc, grad, fisher, importance)
    return (outputs, grad_inner, grad_features, weight_new, fisher_new, importance_new)


def solution(mesh):
    split = Mesh(mesh.devices.reshape(4, 4, 2, mesh.shape["tp"]), ("ctx_0", "ctx_1", "ctx_2", "tp"))
    placed = (
        P(CTX, "tp"),
        P(CTX, "tp"),
        P(CTX, None, "tp"),
        P(CTX, "tp"),
        P("tp"),
        P("tp"),
        P("tp"),
        P(CTX, "tp"),
        P(CTX, None, "tp"),
        P(CTX, None, "tp"),
    )
    return jax.shard_map(
        local,
        mesh=split,
        in_specs=placed,
        out_specs=(
            P(CTX, "tp"),
            P(CTX, "tp"),
            P(CTX, "tp"),
            P(CTX, None, "tp"),
            P(CTX, None, "tp"),
            P(CTX, None, "tp"),
        ),
        check_vma=False,
    )
```

profile of v0, /device:TPU:1, one launch (start us, length us, event | category | flops | bytes accessed | tf_op | source)
XLA Modules:
  0.0 664.1 jit_solution(10560624996359038437)
XLA Ops:
  9.0 1.4 pad_maximum_fusion
  12.3 54.7 %all-gather.17.cloned.1.call-done = bf16[256,8192]{1,0:T(8,128)(2,1)} async-done(((bf16[256,1024]{1,0:T(8,128)(2,1)}), bf16[256,8192]{1,0:T(8,128)(2,1)}) %all-gather.17.cloned.1.call-update) | async-done | bytes 4194320 | tf_op jit(solution)/shard_map/all_gather | solution.py:135
  67.0 143.1 %all-gather.15.cloned.1.call-done = bf16[8192,272]{0,1:T(8,128)(2,1)} async-done(((bf16[256,272]{0,1:T(8,128)(2,1)}), bf16[8192,272]{0,1:T(8,128)(2,1)}) %all-gather.15.cloned.1.call-update) | async-done | bytes 4456464 | tf_op jit(solution)/shard_map/all_gather | solution.py:26
  210.2 3.5 fusion.246
  215.0 4.8 fusion.54
  220.0 1.4 convolution_add_fusion.1
  221.9 1.4 convolution_add_fusion
  226.1 3.8 all-reduce.3
  230.0 6.0 all-reduce.4
  236.6 29.4 %all-gather.27.cloned.1.call-done = f32[32,64,128]{2,1,0:T(8,128)} async-done(((f32[16,64,128]{2,1,0:T(8,128)}), f32[32,64,128]{2,1,0:T(8,128)}) %all-gather.27.cloned.1.call-update) | async-done | bytes 1048592 | tf_op jit(solution)/shard_map/all_gather | solution.py:44
  266.0 2.1 bitcast_add_fusion.30
  268.2 26.9 %all-gather.29.cloned.1.call-done = f32[32,64,128]{2,1,0:T(8,128)} async-done(((f32[16,64,128]{2,1,0:T(8,128)}), f32[32,64,128]{2,1,0:T(8,128)}) %all-gather.29.cloned.1.call-update) | async-done | bytes 1048592 | tf_op jit(solution)/shard_map/all_gather | solution.py:44
  295.1 2.1 bitcast_add_fusion.28
  297.9 33.2 %all-gather.19.cloned.1.call-done = f32[4,1,16,64,128]{4,3,2,1,0:T(8,128)} async-done(((f32[1,1,16,64,128]{4,3,2,1,0:T(8,128)}), f32[4,1,16,64,128]{4,3,2,1,0:T(8,128)}) %all-gather.19.cloned.1.call-update) | async-done | bytes 2097168 | tf_op jit(solution)/shard_map/all_gather | solution.py:44
  331.1 35.6 %all-gather.23.cloned.1.call-done = f32[4,1,16,64,128]{4,3,2,1,0:T(8,128)} async-done(((f32[1,1,16,64,128]{4,3,2,1,0:T(8,128)}), f32[4,1,16,64,128]{4,3,2,1,0:T(8,128)}) %all-gather.23.cloned.1.call-update) | async-done | bytes 2097168 | tf_op jit(solution)/shard_map/all_gather | solution.py:44
  366.8 3.6 multiply_add_fusion
  371.2 2.0 copy.179
  373.3 2.1 copy.192
  378.9 7.6 %all_gather.69 = f32[4,1,16]{2,1,0:T(1,128)S(1)} all-gather(f32[1,1,16]{2,1,0:T(1,128)S(1)} %get-tuple-element.452), channel_id=1, replica_groups=mesh['ctx_0'=4,'ctx_1'=4,'ctx_2'=2,'tp'=8] {'ctx_0'}, dimensions={0}, use_global_device_ids=true | all-gather | bytes 320 | tf_op jit(solution)/shard_map/all_gather | solution.py:44
  386.5 6.5 all_gather.64
  393.0 1.4 convolution_bitcast_fusion.7
  397.8 6.1 all-gather.21.cloned.1.call-done
  403.9 3.0 add_add_fusion
  407.7 1.8 convolution_bitcast_fusion.6
  409.5 30.2 %all-gather.25.cloned.1.call-done = f32[4,1,16,64,128]{4,3,2,1,0:T(8,128)} async-done(((f32[1,1,16,64,128]{4,3,2,1,0:T(8,128)}), f32[4,1,16,64,128]{4,3,2,1,0:T(8,128)}) %all-gather.25.cloned.1.call-update) | async-done | bytes 2097168 | tf_op jit(solution)/shard_map/all_gather | solution.py:44
  439.7 5.4 multiply_reduce_fusion.2
  445.0 1.5 copy.228
  446.5 2.4 fusion.245
  450.0 5.2 fusion.10
  456.0 4.1 fusion.57
  460.1 4.6 convolution_bitcast_fusion
  466.3 7.8 %all-to-all-start.1 = ((bf16[8,1024,16]{1,2,0:T(8,128)(2,1)}), bf16[8,1024,16]{1,2,0:T(8,128)(2,1)S(1)}, u32[]{:S(2)}, u32[]{:S(2)}) async-start(bf16[8,1024,16]{1,2,0:T(8,128)(2,1)} %bitcast.591), calls=%async_computation.1 | async-start | bytes 524288 | tf_op jit(solution)/shard_map/all_to_all | solution.py:141
  474.2 4.6 split.9
  478.7 6.4 copy.208
  485.9 7.3 %all-to-all-start = ((bf16[8,1024,256]{2,1,0:T(8,128)(2,1)}), bf16[8,1024,256]{2,1,0:T(8,128)(2,1)}, u32[]{:S(2)}, u32[]{:S(2)}) async-start(bf16[8,1024,256]{2,1,0:T(8,128)(2,1)} %bitcast.574), calls=%async_computation | async-start | bytes 8388608 | tf_op jit(solution)/shard_map/all_to_all | solution.py:140
  493.2 54.8 %reduce-scatter.4.cloned.1.call-done = f32[2048,256]{0,1:T(8,128)} async-done(((f32[8192,256]{0,1:T(8,128)}), f32[2048,256]{0,1:T(8,128)}) %reduce-scatter.4.cloned.1.call-update) | async-done | bytes 2097168 | tf_op jit(solution)/shard_map/reduce_scatter | solution.py:72
  548.3 1.6 convolution_bitcast_fusion.2
  550.0 2.2 multiply_reduce_fusion.5
  552.2 1.5 copy.197
  553.7 1.5 copy.202
  555.1 1.5 copy.205
  556.6 1.5 copy.198
  558.1 1.5 copy.199
  559.5 1.5 copy.195
  562.9 4.9 multiply_reduce_fusion.8
  569.2 1.6 copy.200
  570.7 3.8 reduce-window.54
  574.5 1.6 copy.203
  576.1 3.8 reduce-window.56
  579.8 1.5 copy.204
  581.3 1.4 slice_reduce_fusion.1
  583.9 1.5 copy.201
  588.0 1.6 copy.206
  589.6 3.8 reduce-window.58
  593.3 1.5 copy.207
  594.8 1.4 slice_reduce_fusion
  599.5 2.0 fusion.206
  602.4 1.6 pad_maximum_fusion.1
  605.2 5.9 fusion.50
  611.2 4.3 fusion.32
  617.8 17.2 %all-gather.31.cloned.1.call-done = bf16[557056]{0:T(1024)(128)(2,1)} async-done(((bf16[69632]{0:T(1024)(128)(2,1)}), bf16[557056]{0:T(1024)(128)(2,1)}) %all-gather.31.cloned.1.call-update) | async-done | bytes 1114128 | tf_op jit(solution)/shard_map/all_gather | solution.py:62
  635.0 1.7 reshape.2054
  638.7 4.6 fusion.47
  643.3 11.1 %reduce-scatter.8.cloned.1.call-done = f32[256,256]{0,1:T(8,128)} async-done(((f32[512,256]{0,1:T(8,128)}), f32[256,256]{0,1:T(8,128)}) %reduce-scatter.8.cloned.1.call-update) | async-done | bytes 262160 | tf_op jit(solution)/shard_map/reduce_scatter | solution.py:72
  (236 shorter events, 40.7 us)
Async XLA Ops:
  7.2 59.9 %all-gather.17.cloned.1.call-start = ((), (), s32[]{:S(2)}) async-start(), calls=%async_computation.6 | async-start | bytes 4718592 | tf_op jit(solution)/shard_map/all_gather | solution.py:135
  7.9 202.3 %all-gather.15.cloned.1.call-start = ((), (), s32[]{:S(2)}) async-start(), calls=%async_computation.5 | async-start | bytes 4595712 | tf_op jit(solution)/shard_map/all_gather | solution.py:26
  10.4 255.6 %all-gather.27.cloned.1.call-start = ((), (), s32[]{:S(2)}) async-start(), calls=%async_computation.14 | async-start | bytes 1572864 | tf_op jit(solution)/shard_map/all_gather | solution.py:44
  11.1 202.6 %copy-start.65 = (f32[16]{0:T(128)}, f32[16]{0:T(128)S(1)}, u32[]{:S(2)}) copy-start(f32[16]{0:T(128)S(1)} %neg.70) | copy-start | bytes 196
  12.3 207.7 %copy-start.5 = (f32[256,1024]{0,1:T(8,128)}, f32[256,1024]{0,1:T(8,128)S(1)}, u32[]{:S(2)}) copy-start(f32[256,1024]{0,1:T(8,128)S(1)} %copy.184) | copy-start | bytes 3145732
  213.7 6.1 copy-start.15
  214.6 231.9 %copy-start.11 = (f32[16,1,2,128]{0,3,2,1:T(8,128)}, f32[16,1,2,128]{0,3,2,1:T(8,128)S(1)}, u32[]{:S(2)}) copy-start(f32[16,1,2,128]{0,3,2,1:T(8,128)S(1)} %copy.180) | copy-start | bytes 49156
  214.7 7.0 %copy-start.19 = (f32[16,1,256]{0,2,1:T(8,128)}, f32[16,1,256]{0,2,1:T(8,128)S(1)}, u32[]{:S(2)}) copy-start(f32[16,1,256]{0,2,1:T(8,128)S(1)} %bitcast_add_fusion.43) | copy-start | bytes 49156
  215.0 6.5 copy-start.2
  219.8 235.7 %copy-start.13 = (bf16[256,256]{0,1:T(8,128)(2,1)}, bf16[256,256]{0,1:T(8,128)(2,1)S(1)}, u32[]{:S(2)}) copy-start(bf16[256,256]{0,1:T(8,128)(2,1)S(1)} %fusion.54) | copy-start | bytes 393220
  220.0 48.2 %copy-start.42 = (f32[256,16]{0,1:T(8,128)}, f32[256,16]{0,1:T(8,128)S(1)}, u32[]{:S(2)}) copy-start(f32[256,16]{0,1:T(8,128)S(1)} %copy.185) | copy-start | bytes 49156
  221.4 73.6 %all-gather.29.cloned.1.call-start = ((), (), s32[]{:S(2)}) async-start(), calls=%async_computation.15 | async-start | bytes 1572864 | tf_op jit(solution)/shard_map/all_gather | solution.py:44
  223.4 107.7 %all-gather.19.cloned.1.call-start = ((), (), s32[]{:S(2)}) async-start(), calls=%async_computation.7 | async-start | bytes 2621440 | tf_op jit(solution)/shard_map/all_gather | solution.py:44
  236.0 130.8 %copy-start.41 = (f32[64]{0:T(128)}, f32[64]{0:T(128)S(1)}, u32[]{:S(2)}) copy-start(f32[64]{0:T(128)S(1)} %all-reduce.4) | copy-start | bytes 772
  236.6 130.1 %copy-start.49 = (f32[16]{0:T(128)}, f32[16]{0:T(128)S(1)}, u32[]{:S(2)}) copy-start(f32[16]{0:T(128)S(1)} %get-tuple-element.454) | copy-start | bytes 196
  236.6 130.1 %copy-start.50 = (f32[16]{0:T(128)}, f32[16]{0:T(128)S(1)}, u32[]{:S(2)}) copy-start(f32[16]{0:T(128)S(1)} %get-tuple-element.456) | copy-start | bytes 196
  236.6 130.1 %copy-start.54 = (f32[16]{0:T(128)}, f32[16]{0:T(128)S(1)}, u32[]{:S(2)}) copy-start(f32[16]{0:T(128)S(1)} %get-tuple-element.455) | copy-start | bytes 196
  236.6 130.1 %copy-start.56 = (f32[16]{0:T(128)}, f32[16]{0:T(128)S(1)}, u32[]{:S(2)}) copy-start(f32[16]{0:T(128)S(1)} %get-tuple-element.457) | copy-start | bytes 196
  268.2 98.6 %all-gather.23.cloned.1.call-start = ((), (), s32[]{:S(2)}) async-start(), calls=%async_computation.9 | async-start | bytes 2621440 | tf_op jit(solution)/shard_map/all_gather | solution.py:44
  297.2 106.7 %all-gather.21.cloned.1.call-start = ((), (), s32[]{:S(2)}) async-start(), calls=%async_computation.8 | async-start | bytes 2621440 | tf_op jit(solution)/shard_map/all_gather | solution.py:44
  366.8 37.2 %copy-start.1 = (f32[4,1,16,64,128]{4,3,2,1,0:T(8,128)S(1)}, f32[4,1,16,64,128]{4,3,2,1,0:T(8,128)}, u32[]{:S(2)}) copy-start(f32[4,1,16,64,128]{4,3,2,1,0:T(8,128)} %all-gather.19.cloned.1.call-done) | copy-start | bytes 6291460
  370.4 69.3 %all-gather.25.cloned.1.call-start = ((), (), s32[]{:S(2)}) async-start(), calls=%async_computation.10 | async-start | bytes 2621440 | tf_op jit(solution)/shard_map/all_gather | solution.py:44
  371.2 176.9 %reduce-scatter.4.cloned.1.call-start = ((), (), s32[]{:S(2)}) async-start(), calls=%async_computation.11 | async-start | bytes 10485760 | tf_op jit(solution)/shard_map/reduce_scatter | solution.py:72
  449.8 5.6 copy-start.24
  449.8 5.6 copy-start.32
  449.9 5.9 copy-start.6
  449.9 5.9 copy-start.10
  449.9 5.9 copy-start.17
  449.9 5.9 copy-start.18
  449.9 5.9 copy-start.43
  449.9 5.9 copy-start.51
  449.9 5.9 copy-start.52
  449.9 5.9 copy-start.55
  449.9 5.9 copy-start.57
  450.0 5.9 copy-start.58
  450.0 5.9 copy-start.59
  450.0 5.9 copy-start.60
  450.0 5.9 copy-start.61
  450.0 5.9 copy-start.63
  450.0 5.9 copy-start.64
  456.0 8.7 %copy-start.22 = (bf16[256,128]{0,1:T(8,128)(2,1)}, bf16[256,128]{0,1:T(8,128)(2,1)S(1)}, u32[]{:S(2)}) copy-start(bf16[256,128]{0,1:T(8,128)(2,1)S(1)} %fusion.55) | copy-start | bytes 196612
  466.3 18.8 %all-to-all-start.1 = ((bf16[8,1024,16]{1,2,0:T(8,128)(2,1)}), bf16[8,1024,16]{1,2,0:T(8,128)(2,1)S(1)}, u32[]{:S(2)}, u32[]{:S(2)}) async-start(bf16[8,1024,16]{1,2,0:T(8,128)(2,1)} %bitcast.591), calls=%async_computation.1 | async-start | bytes 524288 | tf_op jit(solution)/shard_map/all_to_all | solution.py:141
  485.9 62.5 %copy-start.14 = (bf16[256,256]{0,1:T(8,128)(2,1)S(1)}, bf16[256,256]{0,1:T(8,128)(2,1)}, u32[]{:S(2)}) copy-start(bf16[256,256]{0,1:T(8,128)(2,1)} %copy-done.13) | copy-start | bytes 393220
  485.9 152.8 %all-to-all-start = ((bf16[8,1024,256]{2,1,0:T(8,128)(2,1)}), bf16[8,1024,256]{2,1,0:T(8,128)(2,1)}, u32[]{:S(2)}, u32[]{:S(2)}) async-start(bf16[8,1024,256]{2,1,0:T(8,128)(2,1)} %bitcast.574), calls=%async_computation | async-start | bytes 8388608 | tf_op jit(solution)/shard_map/all_to_all | solution.py:140
  493.2 67.8 %copy-start.23 = (bf16[256,128]{0,1:T(8,128)(2,1)S(1)}, bf16[256,128]{0,1:T(8,128)(2,1)}, u32[]{:S(2)}) copy-start(bf16[256,128]{0,1:T(8,128)(2,1)} %copy-done.22) | copy-start | bytes 196612
  493.2 67.8 %copy-start.34 = (bf16[256,128]{0,1:T(8,128)(2,1)S(1)}, bf16[256,128]{0,1:T(8,128)(2,1)}, u32[]{:S(2)}) copy-start(bf16[256,128]{0,1:T(8,128)(2,1)} %copy-done.33) | copy-start | bytes 196612
  493.2 117.9 %reduce-scatter.6.cloned.1.call-start = ((), (), s32[]{:S(2)}) async-start(), calls=%async_computation.12 | async-start | bytes 2621440 | tf_op jit(solution)/shard_map/reduce_scatter | solution.py:72
  548.1 86.9 %all-gather.31.cloned.1.call-start = ((), (), s32[]{:S(2)}) async-start(), calls=%async_computation.16 | async-start | bytes 1253376 | tf_op jit(solution)/shard_map/all_gather | solution.py:62
  562.9 36.6 %copy-start.12 = (f32[16,1,2,128]{0,3,2,1:T(8,128)S(1)}, f32[16,1,2,128]{0,3,2,1:T(8,128)}, u32[]{:S(2)}) copy-start(f32[16,1,2,128]{0,3,2,1:T(8,128)} %copy-done.11) | copy-start | bytes 49156
  562.9 36.6 %copy-start.16 = (f32[256,16]{1,0:T(8,128)S(1)}, f32[256,16]{1,0:T(8,128)}, u32[]{:S(2)}) copy-start(f32[256,16]{1,0:T(8,128)} %copy-done.15) | copy-start | bytes 49156
  567.8 37.3 %copy-start.7 = (f32[256,1024]{0,1:T(8,128)S(1)}, f32[256,1024]{0,1:T(8,128)}, u32[]{:S(2)}) copy-start(f32[256,1024]{0,1:T(8,128)} %copy-done.5) | copy-start | bytes 3145732
  567.8 37.3 %copy-start.9 = (f32[256,1,16,64]{0,3,2,1:T(8,128)S(1)}, f32[256,1,16,64]{0,3,2,1:T(8,128)}, u32[]{:S(2)}) copy-start(f32[256,1,16,64]{0,3,2,1:T(8,128)} %copy-done.8) | copy-start | bytes 3145732
  567.8 37.3 %copy-start.21 = (f32[256,1,16,64]{0,3,2,1:T(8,128)S(1)}, f32[256,1,16,64]{0,3,2,1:T(8,128)}, u32[]{:S(2)}) copy-start(f32[256,1,16,64]{0,3,2,1:T(8,128)} %get-tuple-element.467) | copy-start | bytes 3145732
  604.0 50.4 %reduce-scatter.8.cloned.1.call-start = ((), (), s32[]{:S(2)}) async-start(), calls=%async_computation.13 | async-start | bytes 786432 | tf_op jit(solution)/shard_map/reduce_scatter | solution.py:72
  605.1 6.0 copy-start.37
  605.1 6.0 copy-start.44
  605.2 6.0 copy-start.45
  605.2 6.0 copy-start.46
  605.2 6.0 copy-start.48
  611.2 5.7 copy-start.3
  615.8 21.5 %copy-start.40 = (bf16[8,1024,16]{1,2,0:T(8,128)(2,1)S(1)}, bf16[8,1024,16]{1,2,0:T(8,128)(2,1)}, u32[]{:S(2)}) copy-start(bf16[8,1024,16]{1,2,0:T(8,128)(2,1)} %copy-done.39) | copy-start | bytes 786436
  638.7 17.2 %copy-start.25 = (bf16[256,2,128]{2,1,0:T(2,128)(2,1)S(1)}, bf16[256,2,128]{2,1,0:T(2,128)(2,1)}, u32[]{:S(2)}) copy-start(bf16[256,2,128]{2,1,0:T(2,128)(2,1)} %param.12) | copy-start | bytes 393220
  638.7 17.2 %copy-start.35 = (f32[256,2,128]{2,1,0:T(2,128)S(1)}, f32[256,2,128]{2,1,0:T(2,128)}, u32[]{:S(2)}) copy-start(f32[256,2,128]{2,1,0:T(2,128)} %param.19) | copy-start | bytes 786436
  638.7 17.2 %copy-start.36 = (f32[256,2,128]{2,1,0:T(2,128)S(1)}, f32[256,2,128]{2,1,0:T(2,128)}, u32[]{:S(2)}) copy-start(f32[256,2,128]{2,1,0:T(2,128)} %param.18) | copy-start | bytes 786436
  (19 other events, 72.9 us)
Sparse Core Ops, SparseCore 0:
  9.8 57.1 all-gather.16
  69.3 140.8 all-gather.14
  221.6 44.3 all-gather.26
  268.2 26.8 all-gather.28
  297.3 33.7 all-gather.18
  333.3 33.3 all-gather.22
  370.5 33.3 all-gather.20
  406.3 33.3 all-gather.24
  464.8 83.1 reduce-scatter.3
  550.4 32.0 reduce-scatter.5
  604.1 30.7 all-gather.30
  637.3 17.0 reduce-scatter.7
where the time goes:
time: 666 us; the launch traced here: 664 us
  waiting for transfers between devices  444 us (67%)
  local copies, waits for them, and re-layouts  58.3 us (9%)
  matrix products  55 us (8%)
  other arithmetic  50.5 us (8%)
  blocking collectives  23.8 us (4%)
  between operations  16.6 us (2%)
  starting transfers between devices  16.1 us (2%)
    all_gather x6, waiting for transfers between devices, prefix_by_axis(): pieces = jax.tree.map(lambda part: lax.all_gather(part, axis), running)  161 us
    all_gather x1, waiting for transfers between devices, in_one_piece(): whole = lax.all_gather(both, axis, axis=dim, tiled=True)  143 us
    reduce_scatter x3, waiting for transfers between devices, summed_rows(): x = lax.psum_scatter(x, axis, scatter_dimension=dim, tiled=True)  65.9 us
    all_gather x1, waiting for transfers between devices, local(): whole = lax.all_gather(features, 'tp', axis=1, tiled=True)  54.7 us
    another operation x23, local copies, waits for them, and re-layouts  17.6 us
    all_gather x1, waiting for transfers between devices, gather_together(): lines, at, gathered = (lax.all_gather(ravelled, axis), 0, [])  17.2 us
    another operation x9, other arithmetic  15.8 us
    dot_general x3, matrix products, span_pass(): intra = jnp.einsum('ghij,jghp->ighp', weights, xc, precision=HIGH)  15.4 us
  transfers between devices with their start and end apart: 14, of which 11 were waited for; matrix products, arithmetic and copies ran while one was open for 18% of the time, Pallas kernels for 0%

commit v1 on v0

--- a/solution.py
+++ b/solution.py
@@ -132,7 +132,9 @@
     tokens = features.shape[0]
     groups = w_bc.shape[2] // N
     per_group = HEADS // G
-    whole = lax.all_gather(features, "tp", axis=1, tiled=True)
+    whole = jnp.concatenate(
+        lax.all_to_all(jnp.stack([features] * lax.axis_size("tp")), "tp", 0, 0), axis=1
+    )
     rows_bc, rows_dt = in_one_piece((w_bc, w_dt), CTX, 0, 1)
     depth = rows_bc.shape[0]
     wide = rows_bc.reshape(depth, 2 * groups * N)

time: 666 us -> 682 us (1.024)
  starting transfers between devices: 16.1 us -> 26.1 us
    all_to_all x0 -> x1, waiting for transfers between devices: none -> 132 us  [local(): lax.all_to_all(jnp.stack([features] * lax.axis_size('tp')), 'tp', 0, 0)]
    all_gather x1, waiting for transfers between devices: 143 us -> 73.6 us  [in_one_piece(): whole = lax.all_gather(both, axis, axis=dim, tiled=True)]
    all_gather x1 -> x0, waiting for transfers between devices: 54.7 us -> none  [local(): whole = lax.all_gather(features, 'tp', axis=1, tiled=True)]
    all_to_all x0 -> x1, starting transfers between devices: none -> 10.1 us  [local(): lax.all_to_all(jnp.stack([features] * lax.axis_size('tp')), 'tp', 0, 0)]
    another operation x23 -> x24, local copies, waits for them, and re-layouts: 17.6 us -> 19.8 us
  transfers between devices with their start and end apart: 14 -> 14, of which waited for: 11 -> 11; matrix products, arithmetic and copies ran while one was open for 18% -> 17% of each run, Pallas kernels for 0% -> 0%
where the time goes in v1:
time: 682 us; the launch traced here: 679 us
  waiting for transfers between devices  445 us (65%)
  local copies, waits for them, and re-layouts  61 us (9%)
  matrix products  56.9 us (8%)
  other arithmetic  49.8 us (7%)
  starting transfers between devices  26.1 us (4%)
  blocking collectives  24.2 us (4%)
  between operations  16.3 us (2%)
    all_gather x6, waiting for transfers between devices, prefix_by_axis(): pieces = jax.tree.map(lambda part: lax.all_gather(part, axis), running)  155 us
    all_to_all x1, waiting for transfers between devices, local(): lax.all_to_all(jnp.stack([features] * lax.axis_size('tp')), 'tp', 0, 0)  132 us
    all_gather x1, waiting for transfers between devices, in_one_piece(): whole = lax.all_gather(both, axis, axis=dim, tiled=True)  73.6 us
    reduce_scatter x3, waiting for transfers between devices, summed_rows(): x = lax.psum_scatter(x, axis, scatter_dimension=dim, tiled=True)  66.1 us
    another operation x23, local copies, waits for them, and re-layouts  17.6 us
    all_gather x1, waiting for transfers between devices, gather_together(): lines, at, gathered = (lax.all_gather(ravelled, axis), 0, [])  17.2 us
    another operation x9, other arithmetic  15.8 us
    dot_general x3, matrix products, span_pass(): intra = jnp.einsum('ghij,jghp->ighp', weights, xc, precision=HIGH)  15.4 us
  transfers between devices with their start and end apart: 14, of which 11 were waited for; matrix products, arithmetic and copies ran while one was open for 17% of the time, Pallas kernels for 0%

profile of v1, /device:TPU:1, one launch (start us, length us, event | category | flops | bytes accessed | tf_op | source)
XLA Modules:
  0.0 679.2 jit_solution(15186149813566624386)
XLA Ops:
  10.9 2.2 stack.2
  13.1 10.1 %all-to-all-start = ((bf16[8,256,1024]{1,2,0:T(8,128)(2,1)}), bf16[8,256,1024]{1,2,0:T(8,128)(2,1)}, u32[]{:S(2)}, u32[]{:S(2)}) async-start(bf16[8,256,1024]{1,2,0:T(8,128)(2,1)} %stack.2), calls=%async_computation | async-start | bytes 8388608 | tf_op jit(solution)/shard_map/all_to_all | solution.py:136
  23.5 132.4 %all-to-all-done = bf16[8,256,1024]{1,2,0:T(8,128)(2,1)} async-done(((bf16[8,256,1024]{1,2,0:T(8,128)(2,1)}), bf16[8,256,1024]{1,2,0:T(8,128)(2,1)}, u32[]{:S(2)}, u32[]{:S(2)}) %all-to-all-start) | async-done | bytes 4194336 | tf_op jit(solution)/shard_map/all_to_all | solution.py:136
  155.9 73.6 %all-gather.14.cloned.1.call-done = bf16[8192,272]{0,1:T(8,128)(2,1)} async-done(((bf16[256,272]{0,1:T(8,128)(2,1)}), bf16[8192,272]{0,1:T(8,128)(2,1)}) %all-gather.14.cloned.1.call-update) | async-done | bytes 4456464 | tf_op jit(solution)/shard_map/all_gather | solution.py:26
  229.5 3.6 fusion.246
  234.1 4.8 fusion.54
  239.2 1.4 convolution_add_fusion
  241.7 1.4 convolution_add_fusion.1
  245.8 3.8 all-reduce.3
  249.7 6.3 all-reduce.4
  256.8 22.5 %all-gather.26.cloned.1.call-done = f32[32,64,128]{2,1,0:T(8,128)} async-done(((f32[16,64,128]{2,1,0:T(8,128)}), f32[32,64,128]{2,1,0:T(8,128)}) %all-gather.26.cloned.1.call-update) | async-done | bytes 1048592 | tf_op jit(solution)/shard_map/all_gather | solution.py:44
  279.3 2.1 bitcast_add_fusion.28
  281.5 27.0 %all-gather.24.cloned.1.call-done = f32[32,64,128]{2,1,0:T(8,128)} async-done(((f32[16,64,128]{2,1,0:T(8,128)}), f32[32,64,128]{2,1,0:T(8,128)}) %all-gather.24.cloned.1.call-update) | async-done | bytes 1048592 | tf_op jit(solution)/shard_map/all_gather | solution.py:44
  308.5 2.1 bitcast_add_fusion.30
  311.4 33.1 %all-gather.20.cloned.1.call-done = f32[4,1,16,64,128]{4,3,2,1,0:T(8,128)} async-done(((f32[1,1,16,64,128]{4,3,2,1,0:T(8,128)}), f32[4,1,16,64,128]{4,3,2,1,0:T(8,128)}) %all-gather.20.cloned.1.call-update) | async-done | bytes 2097168 | tf_op jit(solution)/shard_map/all_gather | solution.py:44
  344.5 35.6 %all-gather.16.cloned.1.call-done = f32[4,1,16,64,128]{4,3,2,1,0:T(8,128)} async-done(((f32[1,1,16,64,128]{4,3,2,1,0:T(8,128)}), f32[4,1,16,64,128]{4,3,2,1,0:T(8,128)}) %all-gather.16.cloned.1.call-update) | async-done | bytes 2097168 | tf_op jit(solution)/shard_map/all_gather | solution.py:44
  380.2 3.6 multiply_add_fusion
  384.7 2.0 copy.183
  386.7 2.0 copy.196
  392.3 7.6 %all_gather.65 = f32[4,1,16]{2,1,0:T(1,128)S(1)} all-gather(f32[1,1,16]{2,1,0:T(1,128)S(1)} %get-tuple-element.452), channel_id=1, replica_groups=mesh['ctx_0'=4,'ctx_1'=4,'ctx_2'=2,'tp'=8] {'ctx_0'}, dimensions={0}, use_global_device_ids=true | all-gather | bytes 320 | tf_op jit(solution)/shard_map/all_gather | solution.py:44
  400.0 6.5 all_gather.60
  406.4 1.4 convolution_bitcast_fusion.7
  411.3 6.1 all-gather.18.cloned.1.call-done
  417.4 3.0 add_add_fusion
  421.2 1.8 convolution_bitcast_fusion.6
  423.0 30.2 %all-gather.22.cloned.1.call-done = f32[4,1,16,64,128]{4,3,2,1,0:T(8,128)} async-done(((f32[1,1,16,64,128]{4,3,2,1,0:T(8,128)}), f32[4,1,16,64,128]{4,3,2,1,0:T(8,128)}) %all-gather.22.cloned.1.call-update) | async-done | bytes 2097168 | tf_op jit(solution)/shard_map/all_gather | solution.py:44
  453.2 5.4 multiply_reduce_fusion.2
  458.5 1.5 copy.232
  460.0 2.3 fusion.245
  463.5 5.2 fusion.10
  469.4 3.7 fusion.57
  473.1 6.8 convolution_bitcast_fusion
  481.6 7.8 %all-to-all-start.2 = ((bf16[8,1024,16]{1,2,0:T(8,128)(2,1)}), bf16[8,1024,16]{1,2,0:T(8,128)(2,1)S(1)}, u32[]{:S(2)}, u32[]{:S(2)}) async-start(bf16[8,1024,16]{1,2,0:T(8,128)(2,1)} %bitcast.594), calls=%async_computation.2 | async-start | bytes 524288 | tf_op jit(solution)/shard_map/all_to_all | solution.py:143
  489.4 4.6 split.9
  494.0 6.4 copy.212
  501.1 7.3 %all-to-all-start.1 = ((bf16[8,1024,256]{2,1,0:T(8,128)(2,1)}), bf16[8,1024,256]{2,1,0:T(8,128)(2,1)}, u32[]{:S(2)}, u32[]{:S(2)}) async-start(bf16[8,1024,256]{2,1,0:T(8,128)(2,1)} %bitcast.577), calls=%async_computation.1 | async-start | bytes 8388608 | tf_op jit(solution)/shard_map/all_to_all | solution.py:142
  508.5 54.8 %reduce-scatter.4.cloned.1.call-done = f32[2048,256]{0,1:T(8,128)} async-done(((f32[8192,256]{0,1:T(8,128)}), f32[2048,256]{0,1:T(8,128)}) %reduce-scatter.4.cloned.1.call-update) | async-done | bytes 2097168 | tf_op jit(solution)/shard_map/reduce_scatter | solution.py:72
  563.6 1.6 convolution_bitcast_fusion.2
  565.2 2.2 multiply_reduce_fusion.5
  567.5 1.5 copy.201
  568.9 1.5 copy.206
  570.4 1.5 copy.209
  571.9 1.5 copy.202
  573.3 1.5 copy.203
  574.8 1.5 copy.199
  578.2 4.9 multiply_reduce_fusion.8
  584.4 1.6 copy.204
  586.0 3.8 reduce-window.54
  589.7 1.6 copy.207
  591.3 3.8 reduce-window.56
  595.1 1.5 copy.208
  599.1 1.5 copy.205
  603.3 1.6 copy.210
  604.8 3.8 reduce-window.58
  608.6 1.5 copy.211
  610.1 1.4 slice_reduce_fusion
  614.7 2.0 fusion.206
  617.6 1.6 pad_maximum_fusion.1
  620.4 5.9 fusion.50
  626.4 4.3 fusion.32
  633.0 17.2 %all-gather.28.cloned.1.call-done = bf16[557056]{0:T(1024)(128)(2,1)} async-done(((bf16[69632]{0:T(1024)(128)(2,1)}), bf16[557056]{0:T(1024)(128)(2,1)}) %all-gather.28.cloned.1.call-update) | async-done | bytes 1114128 | tf_op jit(solution)/shard_map/all_gather | solution.py:62
  650.3 1.7 reshape.2064
  654.0 4.6 fusion.47
  658.6 11.2 %reduce-scatter.8.cloned.1.call-done = f32[256,256]{0,1:T(8,128)} async-done(((f32[512,256]{0,1:T(8,128)}), f32[256,256]{0,1:T(8,128)}) %reduce-scatter.8.cloned.1.call-update) | async-done | bytes 262160 | tf_op jit(solution)/shard_map/reduce_scatter | solution.py:72
  (241 shorter events, 42.5 us)
Async XLA Ops:
  7.2 222.3 %all-gather.14.cloned.1.call-start = ((), (), s32[]{:S(2)}) async-start(), calls=%async_computation.6 | async-start | bytes 4595712 | tf_op jit(solution)/shard_map/all_gather | solution.py:26
  13.1 10.1 %copy-start.67 = (f32[16]{0:T(128)S(1)}, f32[16]{0:T(128)}, u32[]{:S(2)}) copy-start(f32[16]{0:T(128)} %param.15) | copy-start | bytes 196
  13.1 10.1 %copy-start.1 = (bf16[256,1024]{1,0:T(8,128)(2,1)S(1)}, bf16[256,1024]{1,0:T(8,128)(2,1)}, u32[]{:S(2)}) copy-start(bf16[256,1024]{1,0:T(8,128)(2,1)} %param.17) | copy-start | bytes 1572868
  13.1 216.4 %copy-start.66 = (f32[16]{0:T(128)S(1)}, f32[16]{0:T(128)}, u32[]{:S(2)}) copy-start(f32[16]{0:T(128)} %param.14) | copy-start | bytes 196
  13.1 142.7 %all-to-all-start = ((bf16[8,256,1024]{1,2,0:T(8,128)(2,1)}), bf16[8,256,1024]{1,2,0:T(8,128)(2,1)}, u32[]{:S(2)}, u32[]{:S(2)}) async-start(bf16[8,256,1024]{1,2,0:T(8,128)(2,1)} %stack.2), calls=%async_computation | async-start | bytes 8388608 | tf_op jit(solution)/shard_map/all_to_all | solution.py:136
  23.2 256.1 %all-gather.26.cloned.1.call-start = ((), (), s32[]{:S(2)}) async-start(), calls=%async_computation.15 | async-start | bytes 1572864 | tf_op jit(solution)/shard_map/all_gather | solution.py:44
  23.2 215.6 %copy-start.65 = (f32[16]{0:T(128)}, f32[16]{0:T(128)S(1)}, u32[]{:S(2)}) copy-start(f32[16]{0:T(128)S(1)} %neg.70) | copy-start | bytes 196
  233.1 7.8 %copy-start.15 = (f32[256,16]{1,0:T(8,128)}, f32[256,16]{1,0:T(8,128)S(1)}, u32[]{:S(2)}) copy-start(f32[256,16]{1,0:T(8,128)S(1)} %get-tuple-element.464) | copy-start | bytes 49156
  234.0 225.9 %copy-start.10 = (f32[16,1,2,128]{0,3,2,1:T(8,128)}, f32[16,1,2,128]{0,3,2,1:T(8,128)S(1)}, u32[]{:S(2)}) copy-start(f32[16,1,2,128]{0,3,2,1:T(8,128)S(1)} %copy.184) | copy-start | bytes 49156
  234.1 6.7 copy-start.14
  238.9 230.1 %copy-start.12 = (bf16[256,256]{0,1:T(8,128)(2,1)}, bf16[256,256]{0,1:T(8,128)(2,1)S(1)}, u32[]{:S(2)}) copy-start(bf16[256,256]{0,1:T(8,128)(2,1)S(1)} %fusion.54) | copy-start | bytes 393220
  239.0 42.5 %copy-start.19 = (f32[16,1,256]{0,2,1:T(8,128)}, f32[16,1,256]{0,2,1:T(8,128)S(1)}, u32[]{:S(2)}) copy-start(f32[16,1,256]{0,2,1:T(8,128)S(1)} %bitcast_add_fusion.43) | copy-start | bytes 49156
  240.7 67.9 %all-gather.24.cloned.1.call-start = ((), (), s32[]{:S(2)}) async-start(), calls=%async_computation.14 | async-start | bytes 1572864 | tf_op jit(solution)/shard_map/all_gather | solution.py:44
  240.9 139.2 %copy-start.4 = (f32[256,1024]{0,1:T(8,128)}, f32[256,1024]{0,1:T(8,128)S(1)}, u32[]{:S(2)}) copy-start(f32[256,1024]{0,1:T(8,128)S(1)} %copy.188) | copy-start | bytes 3145732
  241.7 138.5 %copy-start.42 = (f32[256,16]{0,1:T(8,128)}, f32[256,16]{0,1:T(8,128)S(1)}, u32[]{:S(2)}) copy-start(f32[256,16]{0,1:T(8,128)S(1)} %copy.189) | copy-start | bytes 49156
  243.1 101.4 %all-gather.20.cloned.1.call-start = ((), (), s32[]{:S(2)}) async-start(), calls=%async_computation.9 | async-start | bytes 2621440 | tf_op jit(solution)/shard_map/all_gather | solution.py:44
  256.1 124.1 %copy-start.41 = (f32[64]{0:T(128)}, f32[64]{0:T(128)S(1)}, u32[]{:S(2)}) copy-start(f32[64]{0:T(128)S(1)} %all-reduce.4) | copy-start | bytes 772
  256.7 123.5 %copy-start.49 = (f32[16]{0:T(128)}, f32[16]{0:T(128)S(1)}, u32[]{:S(2)}) copy-start(f32[16]{0:T(128)S(1)} %get-tuple-element.454) | copy-start | bytes 196
  256.7 123.5 %copy-start.50 = (f32[16]{0:T(128)}, f32[16]{0:T(128)S(1)}, u32[]{:S(2)}) copy-start(f32[16]{0:T(128)S(1)} %get-tuple-element.456) | copy-start | bytes 196
  256.7 123.5 %copy-start.54 = (f32[16]{0:T(128)}, f32[16]{0:T(128)S(1)}, u32[]{:S(2)}) copy-start(f32[16]{0:T(128)S(1)} %get-tuple-element.455) | copy-start | bytes 196
  256.8 123.5 %copy-start.56 = (f32[16]{0:T(128)}, f32[16]{0:T(128)S(1)}, u32[]{:S(2)}) copy-start(f32[16]{0:T(128)S(1)} %get-tuple-element.457) | copy-start | bytes 196
  281.5 98.7 %all-gather.16.cloned.1.call-start = ((), (), s32[]{:S(2)}) async-start(), calls=%async_computation.7 | async-start | bytes 2621440 | tf_op jit(solution)/shard_map/all_gather | solution.py:44
  310.7 106.7 %all-gather.18.cloned.1.call-start = ((), (), s32[]{:S(2)}) async-start(), calls=%async_computation.8 | async-start | bytes 2621440 | tf_op jit(solution)/shard_map/all_gather | solution.py:44
  380.2 37.2 %copy-start = (f32[4,1,16,64,128]{4,3,2,1,0:T(8,128)S(1)}, f32[4,1,16,64,128]{4,3,2,1,0:T(8,128)}, u32[]{:S(2)}) copy-start(f32[4,1,16,64,128]{4,3,2,1,0:T(8,128)} %all-gather.16.cloned.1.call-done) | copy-start | bytes 6291460
  383.9 69.3 %all-gather.22.cloned.1.call-start = ((), (), s32[]{:S(2)}) async-start(), calls=%async_computation.10 | async-start | bytes 2621440 | tf_op jit(solution)/shard_map/all_gather | solution.py:44
  384.6 178.7 %reduce-scatter.4.cloned.1.call-start = ((), (), s32[]{:S(2)}) async-start(), calls=%async_computation.11 | async-start | bytes 10485760 | tf_op jit(solution)/shard_map/reduce_scatter | solution.py:72
  463.3 5.9 copy-start.5
  463.3 5.9 copy-start.9
  463.3 5.9 copy-start.17
  463.3 5.9 copy-start.18
  463.4 5.9 copy-start.43
  463.4 5.9 copy-start.51
  463.4 5.9 copy-start.52
  463.4 5.9 copy-start.55
  463.4 5.9 copy-start.57
  463.4 5.9 copy-start.58
  463.4 5.9 copy-start.59
  463.4 5.9 copy-start.60
  463.4 5.9 copy-start.61
  463.4 5.9 copy-start.63
  469.4 10.5 %copy-start.22 = (bf16[256,128]{0,1:T(8,128)(2,1)}, bf16[256,128]{0,1:T(8,128)(2,1)S(1)}, u32[]{:S(2)}) copy-start(bf16[256,128]{0,1:T(8,128)(2,1)S(1)} %fusion.55) | copy-start | bytes 196612
  473.1 6.8 %copy-start.33 = (bf16[256,128]{0,1:T(8,128)(2,1)}, bf16[256,128]{0,1:T(8,128)(2,1)S(1)}, u32[]{:S(2)}) copy-start(bf16[256,128]{0,1:T(8,128)(2,1)S(1)} %fusion.57) | copy-start | bytes 196612
  481.6 18.8 %all-to-all-start.2 = ((bf16[8,1024,16]{1,2,0:T(8,128)(2,1)}), bf16[8,1024,16]{1,2,0:T(8,128)(2,1)S(1)}, u32[]{:S(2)}, u32[]{:S(2)}) async-start(bf16[8,1024,16]{1,2,0:T(8,128)(2,1)} %bitcast.594), calls=%async_computation.2 | async-start | bytes 524288 | tf_op jit(solution)/shard_map/all_to_all | solution.py:143
  501.1 62.5 %copy-start.13 = (bf16[256,256]{0,1:T(8,128)(2,1)S(1)}, bf16[256,256]{0,1:T(8,128)(2,1)}, u32[]{:S(2)}) copy-start(bf16[256,256]{0,1:T(8,128)(2,1)} %copy-done.12) | copy-start | bytes 393220
  501.1 152.8 %all-to-all-start.1 = ((bf16[8,1024,256]{2,1,0:T(8,128)(2,1)}), bf16[8,1024,256]{2,1,0:T(8,128)(2,1)}, u32[]{:S(2)}, u32[]{:S(2)}) async-start(bf16[8,1024,256]{2,1,0:T(8,128)(2,1)} %bitcast.577), calls=%async_computation.1 | async-start | bytes 8388608 | tf_op jit(solution)/shard_map/all_to_all | solution.py:142
  508.4 67.8 %copy-start.23 = (bf16[256,128]{0,1:T(8,128)(2,1)S(1)}, bf16[256,128]{0,1:T(8,128)(2,1)}, u32[]{:S(2)}) copy-start(bf16[256,128]{0,1:T(8,128)(2,1)} %copy-done.22) | copy-start | bytes 196612
  508.4 67.8 %copy-start.34 = (bf16[256,128]{0,1:T(8,128)(2,1)S(1)}, bf16[256,128]{0,1:T(8,128)(2,1)}, u32[]{:S(2)}) copy-start(bf16[256,128]{0,1:T(8,128)(2,1)} %copy-done.33) | copy-start | bytes 196612
  508.4 117.8 %reduce-scatter.6.cloned.1.call-start = ((), (), s32[]{:S(2)}) async-start(), calls=%async_computation.12 | async-start | bytes 2621440 | tf_op jit(solution)/shard_map/reduce_scatter | solution.py:72
  563.3 86.9 %all-gather.28.cloned.1.call-start = ((), (), s32[]{:S(2)}) async-start(), calls=%async_computation.16 | async-start | bytes 1253376 | tf_op jit(solution)/shard_map/all_gather | solution.py:62
  578.1 36.6 %copy-start.11 = (f32[16,1,2,128]{0,3,2,1:T(8,128)S(1)}, f32[16,1,2,128]{0,3,2,1:T(8,128)}, u32[]{:S(2)}) copy-start(f32[16,1,2,128]{0,3,2,1:T(8,128)} %copy-done.10) | copy-start | bytes 49156
  578.1 36.6 %copy-start.16 = (f32[256,16]{1,0:T(8,128)S(1)}, f32[256,16]{1,0:T(8,128)}, u32[]{:S(2)}) copy-start(f32[256,16]{1,0:T(8,128)} %copy-done.15) | copy-start | bytes 49156
  583.0 37.3 %copy-start.6 = (f32[256,1024]{0,1:T(8,128)S(1)}, f32[256,1024]{0,1:T(8,128)}, u32[]{:S(2)}) copy-start(f32[256,1024]{0,1:T(8,128)} %copy-done.4) | copy-start | bytes 3145732
  583.1 37.3 %copy-start.8 = (f32[256,1,16,64]{0,3,2,1:T(8,128)S(1)}, f32[256,1,16,64]{0,3,2,1:T(8,128)}, u32[]{:S(2)}) copy-start(f32[256,1,16,64]{0,3,2,1:T(8,128)} %copy-done.7) | copy-start | bytes 3145732
  583.1 37.3 %copy-start.21 = (f32[256,1,16,64]{0,3,2,1:T(8,128)S(1)}, f32[256,1,16,64]{0,3,2,1:T(8,128)}, u32[]{:S(2)}) copy-start(f32[256,1,16,64]{0,3,2,1:T(8,128)} %get-tuple-element.467) | copy-start | bytes 3145732
  619.2 50.6 %reduce-scatter.8.cloned.1.call-start = ((), (), s32[]{:S(2)}) async-start(), calls=%async_computation.13 | async-start | bytes 786432 | tf_op jit(solution)/shard_map/reduce_scatter | solution.py:72
  620.3 6.0 copy-start.37
  620.4 6.0 copy-start.44
  620.4 6.0 copy-start.45
  620.4 6.0 copy-start.46
  620.4 6.0 copy-start.48
  631.0 21.6 %copy-start.40 = (bf16[8,1024,16]{1,2,0:T(8,128)(2,1)S(1)}, bf16[8,1024,16]{1,2,0:T(8,128)(2,1)}, u32[]{:S(2)}) copy-start(bf16[8,1024,16]{1,2,0:T(8,128)(2,1)} %copy-done.39) | copy-start | bytes 786436
  654.0 17.4 %copy-start.25 = (bf16[256,2,128]{2,1,0:T(2,128)(2,1)S(1)}, bf16[256,2,128]{2,1,0:T(2,128)(2,1)}, u32[]{:S(2)}) copy-start(bf16[256,2,128]{2,1,0:T(2,128)(2,1)} %param.12) | copy-start | bytes 393220
  654.0 17.4 %copy-start.35 = (f32[256,2,128]{2,1,0:T(2,128)S(1)}, f32[256,2,128]{2,1,0:T(2,128)}, u32[]{:S(2)}) copy-start(f32[256,2,128]{2,1,0:T(2,128)} %param.19) | copy-start | bytes 786436
  654.0 17.4 %copy-start.36 = (f32[256,2,128]{2,1,0:T(2,128)S(1)}, f32[256,2,128]{2,1,0:T(2,128)}, u32[]{:S(2)}) copy-start(f32[256,2,128]{2,1,0:T(2,128)} %param.18) | copy-start | bytes 786436
  (21 other events, 87.8 us)
Sparse Core Ops, SparseCore 0:
  10.3 219.1 all-gather.13
  240.8 38.4 all-gather.25
  281.7 26.8 all-gather.23
  310.8 33.7 all-gather.19
  346.8 33.3 all-gather.15
  384.0 33.3 all-gather.17
  419.8 33.3 all-gather.21
  480.1 83.1 reduce-scatter.3
  565.9 32.0 reduce-scatter.5
  619.3 30.8 all-gather.27
  652.8 17.0 reduce-scatter.7
